TPU v7x, 256 devices: a whole 4x4x8 slice. The times are simulated.
256 devices in a mesh: head: 16 (over z, core), tail: 16 (over y, x).
Axes of the slice: x: 4, y: 4, z: 8, core: 2. Of those that a mesh axis runs over, the one named last changes fastest.
Arguments:
- head_emb: bfloat16 [131072, 800], P(('head', 'tail')), may hold values from -48 to 48
- head_state: float32 [131072], P(('head', 'tail')), may hold values from 0.01 to 1
- tail_emb: bfloat16 [64, 128, 800], P('tail'), may hold values from -1.5 to 1.5
- tail_state: float32 [64, 128], P('tail'), may hold values from 0.01 to 1
- relation_emb: bfloat16 [1024, 800], replicated, may hold values from -3.5 to 3.5
- head_rows: int32 [1024, 256], P(('head', 'tail')), may hold values from 0 to 511
- relations: int32 [1024, 256], P(('head', 'tail')), may hold values from 0 to 1023
- tail_offsets: int32 [1024, 256], P(('head', 'tail')), may hold values from 0 to 127
- tail_owner: int32 [1024, 1], P(('head', 'tail')), may hold values from 0 to 15; in each aligned block of 4 rows (0 to 3, 4 to 7, ...) at most 2 rows name the same one
- tail_local: int32 [1024], P(('head', 'tail')), may hold values from 0 to 3
- block_count: int32 [256], P(('head', 'tail')), may hold values from 1 to 4, as said below
- neg_blocks: int32 [8], replicated, may hold values from 0 to 63, as said below
Outputs:
- head_new: bfloat16 [131072, 800], P(('head', 'tail'))
- head_state_new: float32 [131072], P(('head', 'tail'))
- tail_new: bfloat16 [64, 128, 800], P('tail')
- tail_state_new: float32 [64, 128], P('tail')
Inputs may be any that keep to these rules, and one draw needn't show every extreme that they name: `tail_owner`: no tail index owns the tail blocks of more than 2 edge block slots of one device, and in some devices one owns exactly 2. `block_count`: some device has all 4 slots live. `neg_blocks`: distinct tail blocks; the last tail block is always among them.
All inputs are finite; a program needn't handle non-finite values.
Results may differ from a plain program's by a relative error of at most 0.0012.
The roundings to bfloat16 on the way count: a program that leaves them out, or rounds other values in their place, can miss the bound.
Values may be sent and summed in bfloat16 or wider, within the bound.
A program may use at most 128 MiB of HBM per device.

v0:
```python
import math
import jax
import jax.numpy as jnp
from jax import lax
from jax.sharding import PartitionSpec as P

LEARN_RATE = 0.3


def complex_product(left, right):
    half_width = left.shape[-1] // 2
    left_re, left_im = (left[..., :half_width], left[..., half_width:])
    right_re, right_im = (right[..., :half_width], right[..., half_width:])
    return jnp.concatenate(
        [left_re * right_re - left_im * right_im, left_re * right_im + left_im * right_re], axis=-1
    )


def conj_product(left, right):
    half_width = left.shape[-1] // 2
    left_re, left_im = (left[..., :half_width], left[..., half_width:])
    right_re, right_im = (right[..., :half_width], right[..., half_width:])
    return jnp.concatenate(
        [left_re * right_re + left_im * right_im, left_im * right_re - left_re * right_im], axis=-1
    )


def row_adagrad(embedding, adagrad_state, gradient):
    state_next = adagrad_state + jnp.mean(gradient * gradient, axis=-1)
    updated = (
        embedding.astype(jnp.float32) - LEARN_RATE * gradient / jnp.sqrt(state_next)[..., None]
    )
    return (updated.astype(jnp.bfloat16), state_next)


def head_sum(tail_grad):
    return lax.psum(tail_grad, "head")


def per_device(
    head_emb,
    head_state,
    tail_emb,
    tail_state,
    relation_emb,
    head_rows,
    relations,
    tail_offsets,
    tail_owner,
    tail_local,
    block_count,
    neg_blocks,
):
    block_total = tail_local.shape[0]
    edge_count = head_rows.shape[1]
    row_width = head_emb.shape[1]
    span_rows = tail_emb.shape[1]
    owned_blocks = tail_emb.shape[0]
    peer_count = lax.axis_size("tail")
    tail_rank = lax.axis_index("tail")
    capacity = max(2, (2 * block_total + peer_count - 1) // peer_count)
    owner_rank = tail_owner[:, 0]
    positions = jnp.arange(block_total, dtype=jnp.int32)
    same_owner = owner_rank[:, None] == owner_rank[None, :]
    earlier = positions[None, :] < positions[:, None]
    slot_index = jnp.sum((same_owner & earlier).astype(jnp.int32), axis=1)
    slot_place = owner_rank * capacity + slot_index
    global_block = owner_rank * owned_blocks + tail_local
    partition = lax.all_gather(tail_emb, "tail", axis=0, tiled=True)
    chosen = jnp.take(partition, global_block, axis=0)
    mine_ids = neg_blocks - tail_rank * owned_blocks
    is_mine = (mine_ids >= 0) & (mine_ids < owned_blocks)
    own_negs = jnp.where(
        is_mine[:, None, None],
        jnp.take(tail_emb, jnp.clip(mine_ids, 0, owned_blocks - 1), axis=0),
        jnp.zeros((), jnp.bfloat16),
    )
    negatives = lax.psum(own_negs.astype(jnp.float32).astype(jnp.bfloat16), "tail").reshape(
        -1, row_width
    )
    total_edges = block_total * edge_count
    flat_rows = head_rows.reshape(-1)
    block_of = jnp.arange(total_edges, dtype=jnp.int32) // edge_count
    live_mask = (block_of < block_count[0]).astype(jnp.float32)
    tail_index = block_of * span_rows + tail_offsets.reshape(-1)
    tail_vectors = jnp.take(chosen.reshape(-1, row_width), tail_index, axis=0)
    relation_vectors = jnp.take(relation_emb, relations.reshape(-1), axis=0)
    head_vectors = jnp.take(head_emb, flat_rows, axis=0)
    query = complex_product(
        head_vectors.astype(jnp.float32), relation_vectors.astype(jnp.float32)
    ).astype(jnp.bfloat16)
    per_group = math.gcd(block_total, max(1, 512 // edge_count))
    group_rows = per_group * edge_count
    group_count = total_edges // group_rows

    def grouped(values):
        return values.reshape((group_count, group_rows) + values.shape[1:])

    def score_group(neg_total, group_items):
        query_rows, tail_rows, live_rows = group_items
        query_float = query_rows.astype(jnp.float32)
        positive = jnp.sum(query_float * tail_rows.astype(jnp.float32), axis=1)
        negative = lax.dot_general(
            query_rows, negatives, (((1,), (1,)), ((), ())), preferred_element_type=jnp.float32
        )
        largest = jnp.maximum(positive, jnp.max(negative, axis=1))
        pos_exp = jnp.exp(positive - largest)
        neg_exp = jnp.exp(negative - largest[:, None])
        denominator = pos_exp + jnp.sum(neg_exp, axis=1)
        pos_grad = (pos_exp / denominator - 1.0) * live_rows
        neg_grad = (neg_exp / denominator[:, None] * live_rows[:, None]).astype(jnp.bfloat16)
        query_grad = pos_grad[:, None] * tail_rows.astype(jnp.float32) + jnp.dot(
            neg_grad, negatives, preferred_element_type=jnp.float32
        )
        tail_part = pos_grad[:, None] * query_float
        neg_total = neg_total + lax.dot_general(
            neg_grad, query_rows, (((0,), (0,)), ((), ())), preferred_element_type=jnp.float32
        )
        return (neg_total, (query_grad, tail_part))

    neg_start = jnp.zeros((negatives.shape[0], row_width), jnp.float32)
    neg_part, (query_grad, tail_part) = lax.scan(
        score_group, neg_start, (grouped(query), grouped(tail_vectors), grouped(live_mask))
    )
    query_grad = query_grad.reshape(total_edges, row_width)
    tail_part = tail_part.reshape(total_edges, row_width)
    head_grad = (
        jnp.zeros(head_emb.shape, jnp.float32)
        .at[flat_rows]
        .add(conj_product(query_grad, relation_vectors.astype(jnp.float32)))
    )
    block_grad = (
        jnp.zeros((block_total * span_rows, row_width), jnp.float32)
        .at[tail_index]
        .add(tail_part)
        .astype(jnp.bfloat16)
    )
    outgoing = (
        jnp.zeros((peer_count * capacity, span_rows, row_width), jnp.bfloat16)
        .at[slot_place]
        .set(block_grad.reshape(block_total, span_rows, row_width))
    )
    outgoing = outgoing.reshape(peer_count, capacity, span_rows, row_width)
    slot_ids = (
        jnp.zeros((peer_count * capacity,), jnp.int32)
        .at[slot_place]
        .set(tail_local)
        .reshape(peer_count, capacity)
    )
    incoming, incoming_ids = (
        lax.all_to_all(outgoing, "tail", split_axis=0, concat_axis=0, tiled=True),
        lax.all_to_all(slot_ids, "tail", split_axis=0, concat_axis=0, tiled=True),
    )
    which_block = (
        incoming_ids.reshape(-1)[:, None] == jnp.arange(owned_blocks, dtype=jnp.int32)[None, :]
    ).astype(jnp.bfloat16)
    tail_grad = lax.dot_general(
        which_block,
        incoming.reshape(peer_count * capacity, span_rows * row_width),
        (((0,), (0,)), ((), ())),
        preferred_element_type=jnp.float32,
    )
    neg_weights = (
        (mine_ids[:, None] == jnp.arange(owned_blocks, dtype=jnp.int32)[None, :]) & is_mine[:, None]
    ).astype(jnp.float32)
    neg_all = lax.psum(neg_part, ("head", "tail"))
    tail_total = head_sum(tail_grad) + lax.dot_general(
        neg_weights,
        neg_all.reshape(neg_weights.shape[0], span_rows * row_width),
        (((0,), (0,)), ((), ())),
        precision=lax.Precision.HIGHEST,
        preferred_element_type=jnp.float32,
    )
    head_updated, head_state_updated = row_adagrad(head_emb, head_state, head_grad)
    tail_updated, tail_state_updated = row_adagrad(
        tail_emb, tail_state, tail_total.reshape(owned_blocks, span_rows, row_width)
    )
    return (head_updated, head_state_updated, tail_updated, tail_state_updated)


def solution(mesh):
    placed = (
        P(("head", "tail"), None),
        P(("head", "tail")),
        P("tail", None, None),
        P("tail", None),
        P(),
        P(("head", "tail"), None),
        P(("head", "tail"), None),
        P(("head", "tail"), None),
        P(("head", "tail"), None),
        P(("head", "tail")),
        P(("head", "tail")),
        P(),
    )
    return jax.shard_map(
        per_device,
        mesh=mesh,
        in_specs=placed,
        out_specs=(
            P(("head", "tail"), None),
            P(("head", "tail")),
            P("tail", None, None),
            P("tail", None),
        ),
        check_vma=False,
    )
```

profile of v0, /device:TPU:1, one launch (start us, length us, event | category | flops | bytes accessed | tf_op | source)
XLA Modules:
  0.0 729.9 jit_solution(752198037437776522)
XLA Ops:
  7.2 0.7 all-gather.2.cloned.1.call-update
  7.9 0.9 convert_reduce_fusion
  9.5 0.7 scatter_custom_fusion.1
  10.2 0.7 all_to_all.9
  10.9 7.6 %all-to-all-start = ((s32[16,1,2]{2,1,0:T(1,128)}), s32[16,1,2]{2,1,0:T(1,128)S(1)}, u32[]{:S(2)}, u32[]{:S(2)}) async-start(s32[16,1,2]{2,1,0:T(1,128)} %bitcast.13), calls=%async_computation | async-start | bytes 16384 | tf_op jit(solution)/shard_map/all_to_all | solution.py:152
  19.2 0.9 gather_fusion.1
  20.1 1.4 select_select_fusion
  21.5 3.8 copy.82
  26.1 3.1 copy.79
  29.3 5.3 gather_fusion.3
  34.5 5.3 gather_fusion
  39.8 2.5 select_convert_fusion
  42.4 1.5 subtract_convert_fusion
  44.2 1.2 copy.80
  45.4 1.2 copy.81
  47.3 1.3 pad_maximum_fusion
  48.7 62.8 %all-gather.2.cloned.1.call-done = bf16[64,128,800]{1,2,0:T(8,128)(2,1)} async-done(((bf16[4,128,800]{1,2,0:T(8,128)(2,1)}), bf16[64,128,800]{1,2,0:T(8,128)(2,1)}) %all-gather.2.cloned.1.call-update) | async-done | bytes 13107216 | tf_op jit(solution)/shard_map/all_gather | solution.py:69
  111.5 5.4 gather_fusion.2
  117.0 1.3 copy.83
  118.2 1.4 bitcast_select_fusion
  119.6 5.3 gather_fusion.4
  124.9 3.3 broadcast_select_fusion
  128.2 3.5 copy.84
  131.6 81.5 %all-reduce.4.cloned.1.call-done = bf16[1024,800]{1,0:T(8,128)(2,1)} async-done(((bf16[1024,800]{1,0:T(8,128)(2,1)}), bf16[1024,800]{1,0:T(8,128)(2,1)}) %all-reduce.4.cloned.1.call-update) | async-done | bytes 1638416 | tf_op jit(solution)/shard_map/psum | solution.py:78
  213.2 30.7 %while.17 = (s32[]{:T(128)}, f32[1024,800]{0,1:T(8,128)}, f32[2,512,800]{1,2,0:T(8,128)}, f32[2,512,800]{1,2,0:T(8,128)}, bf16[2,512,800]{1,2,0:T(8,128)(2,1)S(1...) while((s32[]{:T(128)}, f32[1024,800]{0,1:T(8,128)}, ...), condition=%wide.region_5.7_spmd.clone, body=%wide.region_1.6_spmd.clone.sunk | while | flops 2527675904 | bytes 74365712 | solution.py:122
  213.2 3.0 fusion.55
  217.1 1.8 copy-done.7
  218.9 1.4 fusion.58
  220.3 1.8 copy-done.8
  222.1 1.5 multiply_dynamic-update-slice_fusion.2
  223.6 4.5 select_add_fusion.2
  228.1 3.0 fusion.55
  232.0 1.8 copy-done.7
  233.8 1.4 fusion.58
  235.3 1.8 copy-done.8
  237.0 1.4 multiply_dynamic-update-slice_fusion.2
  238.4 5.4 select_add_fusion.2
  243.9 4.4 copy.95
  248.2 10.8 %scatter_custom_fusion.2 = f32[512,800]{1,0:T(8,128)S(1)} fusion(s32[1024]{0:T(1024)S(1)} %bitcast.112, f32[1024,800]{1,0:T(8,128)} %bitcast.92, f32[]{:T(128)} %constant.133.clone.1), kind=kCustom, calls=%fused_computation.49 | custom fusion | flops 819200 | bytes 1638912 | tf_op jit(solution)/shard_map/scatter-add | solution.py:135
  259.1 1.1 convert_element_type.70
  260.2 1.5 copy.90
  261.7 3.6 broadcast_in_dim.108
  265.3 2.8 scatter_fusion
  268.1 4.6 all-to-all-start.1
  272.8 4.9 copy.92
  277.7 6.1 reshape.276
  283.8 1.1 copy-done.4
  284.9 1.3 copy.86
  287.4 4.4 copy.85
  291.8 75.6 %all-to-all-done.1 = bf16[16,2,128,800]{2,3,1,0:T(8,128)(2,1)} async-done(((bf16[16,2,128,800]{2,3,1,0:T(8,128)(2,1)}), bf16[16,2,128,800]{2,3,1,0:T(8,128)(2,1)}, u32[]{:S(2)}, u32[]{:S(2)}) %all-to-all-start.1) | async-done | bytes 6553632 | tf_op jit(solution)/shard_map/all_to_all | solution.py:151
  367.4 11.0 %copy.91 = bf16[16,2,128,800]{3,2,1,0:T(8,128)(2,1)} copy(bf16[16,2,128,800]{2,3,1,0:T(8,128)(2,1)} %all-to-all-done.1) | data formatting | bytes 13107200 | tf_op jit(solution)/shard_map/all_to_all | solution.py:151
  378.5 13.6 %reshape.275 = bf16[32,102400]{1,0:T(8,128)(2,1)} reshape(bf16[16,2,128,800]{3,2,1,0:T(8,128)(2,1)} %copy.91) | data formatting | bytes 13107200 | tf_op jit(solution)/shard_map/reshape | solution.py:159
  392.1 5.1 fusion.20
  397.3 6.6 multiply_add_fusion
  403.9 10.9 %scatter_custom_fusion = f32[512,800]{1,0:T(8,128)S(1)} fusion(s32[1024]{0:T(1024)S(1)} %bitcast.113, f32[1024,400]{1,0:T(8,128)} %get-tuple-element.225, f32[]{:T(128)} %constant.164, f32[1024,400]{1,0:T(8,128)} %get-tuple-element.224, f32[]{:T(128)} %constant.133.clone.1), kind=kCustom, calls=%fused_computation.32 | custom fusion | flops 1638400 | bytes 4915208 | tf_op jit(solution)/shard_map/scatter-add | solution.py:130
  415.5 1.4 subtract_convert_fusion.2
  417.0 2.1 copy.93
  419.1 172.2 %all-reduce.8.cloned.1.call-done = f32[8,102400]{1,0:T(8,128)} async-done(((f32[8,102400]{1,0:T(8,128)}), f32[8,102400]{1,0:T(8,128)}) %all-reduce.8.cloned.1.call-update) | async-done | bytes 3276816 | tf_op jit(solution)/shard_map/psum | solution.py:166
  591.3 116.5 %all-reduce.6.cloned.1.call-done = f32[4,102400]{1,0:T(4,128)} async-done(((f32[4,102400]{1,0:T(4,128)}), f32[4,102400]{1,0:T(4,128)}) %all-reduce.6.cloned.1.call-update) | async-done | bytes 1638416 | tf_op jit(solution)/shard_map/psum | solution.py:37
  707.9 5.1 broadcast_multiply_fusion
  713.0 3.0 mul.159
  716.2 3.1 mul.157
  719.8 1.3 subtract_convert_fusion.1
  721.1 2.2 copy.94
  (93 shorter events, 7.2 us)
Async XLA Ops:
  7.2 12.1 %copy-start.3 = (bf16[4,128,800]{1,2,0:T(8,128)(2,1)S(1)}, bf16[4,128,800]{1,2,0:T(8,128)(2,1)}, u32[]{:S(2)}) copy-start(bf16[4,128,800]{1,2,0:T(8,128)(2,1)} %param.18) | copy-start | bytes 2457604
  7.2 104.3 %all-gather.2.cloned.1.call-start = ((), (), s32[]{:S(2)}) async-start(), calls=%async_computation.3 | async-start | bytes 13926400 | tf_op jit(solution)/shard_map/all_gather | solution.py:69
  10.9 257.2 %all-to-all-start = ((s32[16,1,2]{2,1,0:T(1,128)}), s32[16,1,2]{2,1,0:T(1,128)S(1)}, u32[]{:S(2)}, u32[]{:S(2)}) async-start(s32[16,1,2]{2,1,0:T(1,128)} %bitcast.13), calls=%async_computation | async-start | bytes 16384 | tf_op jit(solution)/shard_map/all_to_all | solution.py:152
  18.5 194.7 %all-reduce.4.cloned.1.call-start = ((), (), s32[]{:S(2)}) async-start(), calls=%async_computation.2 | async-start | bytes 3670016 | tf_op jit(solution)/shard_map/psum | solution.py:78
  21.5 3.8 copy-start.12
  21.5 3.9 copy-start.15
  21.5 3.9 copy-start.16
  21.5 3.9 copy-start.9
  26.1 3.1 copy-start.10
  42.4 1.8 copy-start.1
  44.2 3.1 copy-start.11
  45.4 1.9 copy-start.6
  213.2 3.1 copy-start.2
  213.2 3.9 copy-start.17
  216.2 4.1 copy-start
  216.2 2.7 copy-start.7
  220.3 1.8 copy-start.8
  228.1 3.1 copy-start.2
  228.1 3.9 copy-start.17
  231.1 4.1 copy-start
  231.1 2.7 copy-start.7
  235.2 1.8 copy-start.8
  268.1 99.3 %all-to-all-start.1 = ((bf16[16,2,128,800]{2,3,1,0:T(8,128)(2,1)}), bf16[16,2,128,800]{2,3,1,0:T(8,128)(2,1)}, u32[]{:S(2)}, u32[]{:S(2)}) async-start(bf16[16,2,128,800]{2,3,1,0:T(8,128)(2,1)} %bitcast.86), calls=%async_computation.1 | async-start | bytes 13107200 | tf_op jit(solution)/shard_map/all_to_all | solution.py:151
  272.7 318.6 %all-reduce.8.cloned.1.call-start = ((), (), s32[]{:S(2)}) async-start(), calls=%async_computation.5 | async-start | bytes 6553600 | tf_op jit(solution)/shard_map/psum | solution.py:166
  283.7 1.1 copy-start.4
  283.7 424.1 %all-reduce.6.cloned.1.call-start = ((), (), s32[]{:S(2)}) async-start(), calls=%async_computation.4 | async-start | bytes 3276800 | tf_op jit(solution)/shard_map/psum | solution.py:37
  403.9 11.1 %copy-start.13 = (f32[512]{0:T(512)S(1)}, f32[512]{0:T(512)}, u32[]{:S(2)}) copy-start(f32[512]{0:T(512)} %param.17) | copy-start | bytes 6148
  716.1 3.1 copy-start.14
  716.2 3.7 copy-start.5
Sparse Core Ops, SparseCore 0:
  10.4 101.0 all-gather.1
  114.9 98.2 all-reduce.3
  283.9 307.4 all-reduce.7
  593.6 114.2 all-reduce.5
where the time goes:
time: 731 us; the launch traced here: 730 us
  waiting for transfers between devices  509 us (70%)
  local copies, waits for them, and re-layouts  111 us (15%)
  other arithmetic  52.5 us (7%)
  matrix products  29.1 us (4%)
  between operations  14.8 us (2%)
  starting transfers between devices  12.4 us (2%)
    psum x1, waiting for transfers between devices, per_device(): neg_all = lax.psum(neg_part, ('head', 'tail'))  172 us
    psum x1, waiting for transfers between devices, head_sum(): return lax.psum(tail_grad, 'head')  117 us
    psum x1, waiting for transfers between devices, per_device(): lax.psum(own_negs.astype(jnp.float32).astype(jnp.bfloat16), 'tail')  81.5 us
    all_to_all x1, waiting for transfers between devices, per_device(): lax.all_to_all(outgoing, 'tail', split_axis=0, concat_axis=0, tiled=True)  75.6 us
    all_gather x1, waiting for transfers between devices, per_device(): partition = lax.all_gather(tail_emb, 'tail', axis=0, tiled=True)  62.8 us
  transfers between devices with their start and end apart: 6, of which 5 were waited for; matrix products, arithmetic and copies ran while one was open for 23% of the time, Pallas kernels for 0%

commit v1 on v0

--- a/solution.py
+++ b/solution.py
@@ -66,7 +66,20 @@
     slot_index = jnp.sum((same_owner & earlier).astype(jnp.int32), axis=1)
     slot_place = owner_rank * capacity + slot_index
     global_block = owner_rank * owned_blocks + tail_local
-    partition = lax.all_gather(tail_emb, "tail", axis=0, tiled=True)
+    how_many = lax.axis_size("tail")
+    pool = tuple(((no, (no + 1) % how_many) for no in range(how_many)))
+    o_now, next_value = ([tail_emb], [tail_emb])
+    so_far_all = tuple(((no, (no - 1) % how_many) for no in range(how_many)))
+    for _ in range(how_many // 2):
+        o_now.append(lax.ppermute(o_now[-1], "tail", pool))
+    dd = 0
+    while dd < (how_many - 1) // 2:
+        next_value.append(lax.ppermute(next_value[-1], "tail", so_far_all))
+        dd = dd + 1
+    frame_out = jnp.concatenate([*o_now[::-1], *next_value[1:]], axis=0)
+    partition = jnp.roll(
+        frame_out, (lax.axis_index("tail") - how_many // 2) * tail_emb.shape[0], axis=0
+    )
     chosen = jnp.take(partition, global_block, axis=0)
     mine_ids = neg_blocks - tail_rank * owned_blocks
     is_mine = (mine_ids >= 0) & (mine_ids < owned_blocks)

time: 731 us -> 773 us (1.057); the launches traced: 730 us -> 763 us
  starting transfers between devices: 12.4 us -> 50.5 us
  waiting for transfers between devices: 509 us -> 475 us
  local copies, waits for them, and re-layouts: 111 us -> 143 us
    ppermute x0 -> x15, waiting for transfers between devices: none -> 86.6 us  [the longest x8 64.1 us: per_device(): o_now.append(lax.ppermute(o_now[-1], 'tail', pool))]
    all_gather x1 -> x0, waiting for transfers between devices: 62.8 us -> none  [per_device(): partition = lax.all_gather(tail_emb, 'tail', axis=0, tiled=True)]
    psum x1, waiting for transfers between devices: 81.5 us -> 23.3 us  [per_device(): lax.psum(own_negs.astype(jnp.float32).astype(jnp.bfloat16), 'tail')]
    ppermute x0 -> x15, starting transfers between devices: none -> 37.1 us  [the longest x7 34.8 us: per_device(): next_value.append(lax.ppermute(next_value[-1], 'tail', so_far_all))]
    unnamed x38 -> x81, local copies, waits for them, and re-layouts: 14.2 us -> 38.8 us
  transfers between devices with their start and end apart: 6 -> 20, of which waited for: 5 -> 14; matrix products, arithmetic and copies ran while one was open for 23% -> 26% of each run, Pallas kernels for 0% -> 0%
where the time goes in v1:
time: 773 us; the launch traced here: 763 us
  waiting for transfers between devices  475 us (61%)
  local copies, waits for them, and re-layouts  143 us (18%)
  other arithmetic  50.6 us (7%)
  starting transfers between devices  50.5 us (7%)
  matrix products  29 us (4%)
  between operations  15.3 us (2%)
    psum x1, waiting for transfers between devices, per_device(): neg_all = lax.psum(neg_part, ('head', 'tail'))  173 us
    psum x1, waiting for transfers between devices, head_sum(): return lax.psum(tail_grad, 'head')  117 us
    all_to_all x1, waiting for transfers between devices, per_device(): lax.all_to_all(outgoing, 'tail', split_axis=0, concat_axis=0, tiled=True)  75 us
    ppermute x8, waiting for transfers between devices, per_device(): o_now.append(lax.ppermute(o_now[-1], 'tail', pool))  64.1 us
    unnamed x81, local copies, waits for them, and re-layouts  38.8 us
    ppermute x7, starting transfers between devices, per_device(): next_value.append(lax.ppermute(next_value[-1], 'tail', so_far_all))  34.8 us
    psum x1, waiting for transfers between devices, per_device(): lax.psum(own_negs.astype(jnp.float32).astype(jnp.bfloat16), 'tail')  23.3 us
    ppermute x7, waiting for transfers between devices, per_device(): next_value.append(lax.ppermute(next_value[-1], 'tail', so_far_all))  22.5 us
  transfers between devices with their start and end apart: 20, of which 14 were waited for; matrix products, arithmetic and copies ran while one was open for 26% of the time, Pallas kernels for 0%

profile of v1, /device:TPU:1, one launch (start us, length us, event | category | flops | bytes accessed | tf_op | source)
XLA Modules:
  0.0 762.8 jit_solution(9563556101656185148)
XLA Ops:
  7.2 2.1 collective-permute-start
  9.3 20.0 %collective-permute-done = bf16[4,128,800]{1,2,0:T(8,128)(2,1)S(1)} collective-permute-done((bf16[4,128,800]{1,2,0:T(8,128)(2,1)}, bf16[4,128,800]{1,2,0:T(8,128)(2,1)S(1)}, u32[]{:S(2)}, u32[]{:S(2)}) %collective-permute-start) | collective-permute-done | bytes 819232 | tf_op jit(solution)/shard_map/ppermute | solution.py:74
  29.4 4.8 collective-permute-start.8
  34.1 15.2 %collective-permute-done.1 = bf16[4,128,800]{1,2,0:T(8,128)(2,1)S(1)} collective-permute-done((bf16[4,128,800]{1,2,0:T(8,128)(2,1)S(1)}, bf16[4,128,800]{1,2,0:T(8,128)(2,1)S(1)}, u32[]{:S(2)}, u32[]{:S(2)}) %collective-permute-start.1) | collective-permute-done | bytes 819232 | tf_op jit(solution)/shard_map/ppermute | solution.py:74
  50.8 4.9 collective-permute-start.9
  55.6 13.1 %collective-permute-done.2 = bf16[4,128,800]{1,2,0:T(8,128)(2,1)} collective-permute-done((bf16[4,128,800]{1,2,0:T(8,128)(2,1)S(1)}, bf16[4,128,800]{1,2,0:T(8,128)(2,1)}, u32[]{:S(2)}, u32[]{:S(2)}) %collective-permute-start.2) | collective-permute-done | bytes 819232 | tf_op jit(solution)/shard_map/ppermute | solution.py:74
  68.7 2.0 gather_fusion.1
  70.7 1.5 select_select_fusion
  72.2 3.8 copy.82
  76.3 4.9 collective-permute-start.10
  81.1 6.2 collective-permute-done.3
  88.6 8.6 %all-to-all-start = ((s32[16,1,2]{2,1,0:T(1,128)}), s32[16,1,2]{2,1,0:T(1,128)S(1)}, u32[]{:S(2)}, u32[]{:S(2)}) async-start(s32[16,1,2]{2,1,0:T(1,128)} %bitcast.13), calls=%async_computation | async-start | bytes 16384 | tf_op jit(solution)/shard_map/all_to_all | solution.py:165
  97.4 4.8 collective-permute-start.11
  102.1 5.4 collective-permute-done.4
  108.2 3.0 copy.79
  111.3 5.3 gather_fusion.3
  116.5 5.3 gather_fusion
  121.8 1.9 select_convert_fusion
  124.2 4.8 collective-permute-start.12
  129.2 1.5 subtract_convert_fusion
  133.1 5.5 collective-permute-done.12
  138.6 5.2 collective-permute-start.13
  143.9 2.9 collective-permute-done.6
  148.1 14.5 %collective-permute-done.13 = bf16[4,128,800]{1,2,0:T(8,128)(2,1)S(1)} collective-permute-done((bf16[4,128,800]{1,2,0:T(8,128)(2,1)}, bf16[4,128,800]{1,2,0:T(8,128)(2,1)S(1)}, u32[]{:S(2)}, u32[]{:S(2)}) %collective-permute-start.13) | collective-permute-done | bytes 819232 | tf_op jit(solution)/shard_map/ppermute | solution.py:77
  162.5 5.5 collective-permute-start.14
  181.6 2.5 collective-permute-done.14
  196.3 5.6 constant_dynamic-slice_fusion.1
  202.0 5.5 gather_fusion.2
  210.1 5.3 gather_fusion.4
  215.4 3.1 broadcast_select_fusion
  218.4 3.5 copy.84
  221.9 23.3 %all-reduce.4.cloned.1.call-done = bf16[1024,800]{1,0:T(8,128)(2,1)} async-done(((bf16[1024,800]{1,0:T(8,128)(2,1)}), bf16[1024,800]{1,0:T(8,128)(2,1)}) %all-reduce.4.cloned.1.call-update) | async-done | bytes 1638416 | tf_op jit(solution)/shard_map/psum | solution.py:91
  245.3 30.6 %while.17 = (s32[]{:T(128)}, f32[1024,800]{0,1:T(8,128)}, f32[2,512,800]{1,2,0:T(8,128)}, f32[2,512,800]{1,2,0:T(8,128)}, bf16[2,512,800]{1,2,0:T(8,128)(2,1)S(1...) while((s32[]{:T(128)}, f32[1024,800]{0,1:T(8,128)}, ...), condition=%wide.region_5.7_spmd.clone, body=%wide.region_1.0_spmd.clone.sunk | while | flops 2527675904 | bytes 74365712 | solution.py:135
  245.3 3.0 fusion.55
  249.2 1.8 copy-done.13
  251.0 1.4 fusion.58
  252.5 1.8 copy-done.14
  255.7 4.4 select_add_fusion.2
  260.1 3.0 fusion.55
  264.0 1.8 copy-done.13
  267.3 1.8 copy-done.14
  270.5 5.4 select_add_fusion.2
  275.9 4.4 copy.95
  280.3 10.7 %scatter_custom_fusion.2 = f32[512,800]{1,0:T(8,128)S(1)} fusion(s32[1024]{0:T(1024)S(1)} %bitcast.112, f32[1024,800]{1,0:T(8,128)} %bitcast.92, f32[]{:T(128)} %constant.153.clone.1), kind=kCustom, calls=%fused_computation.49 | custom fusion | flops 819200 | bytes 1638912 | tf_op jit(solution)/shard_map/scatter-add | solution.py:148
  292.0 1.5 copy.90
  293.6 3.6 broadcast_in_dim.108
  297.1 2.7 scatter_fusion
  299.9 4.6 all-to-all-start.1
  304.6 5.3 copy.92
  309.9 6.0 reshape.276
  319.6 4.4 copy.85
  324.0 75.0 %all-to-all-done.1 = bf16[16,2,128,800]{2,3,1,0:T(8,128)(2,1)} async-done(((bf16[16,2,128,800]{2,3,1,0:T(8,128)(2,1)}), bf16[16,2,128,800]{2,3,1,0:T(8,128)(2,1)}, u32[]{:S(2)}, u32[]{:S(2)}) %all-to-all-start.1) | async-done | bytes 6553632 | tf_op jit(solution)/shard_map/all_to_all | solution.py:164
  399.1 11.0 %copy.91 = bf16[16,2,128,800]{3,2,1,0:T(8,128)(2,1)} copy(bf16[16,2,128,800]{2,3,1,0:T(8,128)(2,1)} %all-to-all-done.1) | data formatting | bytes 13107200 | tf_op jit(solution)/shard_map/all_to_all | solution.py:164
  410.1 13.6 %reshape.275 = bf16[32,102400]{1,0:T(8,128)(2,1)} reshape(bf16[16,2,128,800]{3,2,1,0:T(8,128)(2,1)} %copy.91) | data formatting | bytes 13107200 | tf_op jit(solution)/shard_map/reshape | solution.py:172
  423.7 5.2 fusion.20
  428.9 6.7 multiply_add_fusion
  435.5 11.0 %scatter_custom_fusion = f32[512,800]{1,0:T(8,128)S(1)} fusion(s32[1024]{0:T(1024)S(1)} %bitcast.113, f32[1024,400]{1,0:T(8,128)} %get-tuple-element.225, f32[]{:T(128)} %constant.186, f32[1024,400]{1,0:T(8,128)} %get-tuple-element.224, f32[]{:T(128)} %constant.153.clone.1), kind=kCustom, calls=%fused_computation.32 | custom fusion | flops 1638400 | bytes 4915208 | tf_op jit(solution)/shard_map/scatter-add | solution.py:143
  448.7 2.1 copy.93
  450.9 173.0 %all-reduce.8.cloned.1.call-done = f32[8,102400]{1,0:T(8,128)} async-done(((f32[8,102400]{1,0:T(8,128)}), f32[8,102400]{1,0:T(8,128)}) %all-reduce.8.cloned.1.call-update) | async-done | bytes 3276816 | tf_op jit(solution)/shard_map/psum | solution.py:179
  623.9 116.7 %all-reduce.6.cloned.1.call-done = f32[4,102400]{1,0:T(4,128)} async-done(((f32[4,102400]{1,0:T(4,128)}), f32[4,102400]{1,0:T(4,128)}) %all-reduce.6.cloned.1.call-update) | async-done | bytes 1638416 | tf_op jit(solution)/shard_map/psum | solution.py:37
  740.5 5.1 broadcast_multiply_fusion
  745.7 3.0 mul.163
  748.9 3.1 mul.161
  753.9 2.2 copy.94
  (164 shorter events, 50.4 us)
Async XLA Ops:
  7.2 238.1 %all-reduce.4.cloned.1.call-start = ((), (), s32[]{:S(2)}) async-start(), calls=%async_computation.2 | async-start | bytes 3670016 | tf_op jit(solution)/shard_map/psum | solution.py:91
  7.2 22.1 %collective-permute-start = (bf16[4,128,800]{1,2,0:T(8,128)(2,1)}, bf16[4,128,800]{1,2,0:T(8,128)(2,1)S(1)}, u32[]{:S(2)}, u32[]{:S(2)}) collective-permute-start(bf16[4,128,800]{1,2,0:T(8,128)(2,1)} %param.18), channel_id=1, source_target_pairs={{0,1},{1,2},{2,3},{3,4},{4,5},{5,6},{6,7},{7,8},{8,9},{9,10},{10,1... | collective-permute-start | bytes 2457608 | tf_op jit(solution)/shard_map/ppermute | solution.py:74
  29.4 42.8 %copy-start.7 = (bf16[4,128,800]{1,2,0:T(8,128)(2,1)}, bf16[4,128,800]{1,2,0:T(8,128)(2,1)S(1)}, u32[]{:S(2)}) copy-start(bf16[4,128,800]{1,2,0:T(8,128)(2,1)S(1)} %collective-permute-done) | copy-start | bytes 2457604
  29.4 20.0 %collective-permute-start.1 = (bf16[4,128,800]{1,2,0:T(8,128)(2,1)S(1)}, bf16[4,128,800]{1,2,0:T(8,128)(2,1)S(1)}, u32[]{:S(2)}, u32[]{:S(2)}) collective-permute-start(bf16[4,128,800]{1,2,0:T(8,128)(2,1)S(1)} %collective-permute-done), channel_id=1, source_target_pairs={{0,1},{1,2},{2,3},{3,4},{4,5},{5,6},{6,7},{7,8},{8,9},{9,10},{10,1... | collective-permute-start | bytes 2457608 | tf_op jit(solution)/shard_map/ppermute | solution.py:74
  29.4 21.4 %collective-permute-start.8 = (bf16[4,128,800]{1,2,0:T(8,128)(2,1)}, bf16[4,128,800]{1,2,0:T(8,128)(2,1)S(1)}, u32[]{:S(2)}, u32[]{:S(2)}) collective-permute-start(bf16[4,128,800]{1,2,0:T(8,128)(2,1)} %param.18), channel_id=1, source_target_pairs={{0,15},{1,0},{2,1},{3,2},{4,3},{5,4},{6,5},{7,6},{8,7},{9,8},{10,9... | collective-permute-start | bytes 2457608 | tf_op jit(solution)/shard_map/ppermute | solution.py:77
  49.4 19.3 %copy-start.11 = (bf16[4,128,800]{1,2,0:T(8,128)(2,1)}, bf16[4,128,800]{1,2,0:T(8,128)(2,1)S(1)}, u32[]{:S(2)}) copy-start(bf16[4,128,800]{1,2,0:T(8,128)(2,1)S(1)} %collective-permute-done.1) | copy-start | bytes 2457604
  49.4 19.3 %collective-permute-start.2 = (bf16[4,128,800]{1,2,0:T(8,128)(2,1)S(1)}, bf16[4,128,800]{1,2,0:T(8,128)(2,1)}, u32[]{:S(2)}, u32[]{:S(2)}) collective-permute-start(bf16[4,128,800]{1,2,0:T(8,128)(2,1)S(1)} %collective-permute-done.1), channel_id=1, source_target_pairs={{0,1},{1,2},{2,3},{3,4},{4,5},{5,6},{6,7},{7,8},{8,9},{9,10},{10,1... | collective-permute-start | bytes 2457608 | tf_op jit(solution)/shard_map/ppermute | solution.py:74
  50.8 21.4 %copy-start.9 = (bf16[4,128,800]{1,2,0:T(8,128)(2,1)}, bf16[4,128,800]{1,2,0:T(8,128)(2,1)S(1)}, u32[]{:S(2)}) copy-start(bf16[4,128,800]{1,2,0:T(8,128)(2,1)S(1)} %collective-permute-done.8) | copy-start | bytes 2457604
  50.8 25.5 %collective-permute-start.9 = (bf16[4,128,800]{1,2,0:T(8,128)(2,1)S(1)}, bf16[4,128,800]{1,2,0:T(8,128)(2,1)}, u32[]{:S(2)}, u32[]{:S(2)}) collective-permute-start(bf16[4,128,800]{1,2,0:T(8,128)(2,1)S(1)} %collective-permute-done.8), channel_id=1, source_target_pairs={{0,15},{1,0},{2,1},{3,2},{4,3},{5,4},{6,5},{7,6},{8,7},{9,8},{10,9... | collective-permute-start | bytes 2457608 | tf_op jit(solution)/shard_map/ppermute | solution.py:77
  68.7 18.6 %collective-permute-start.3 = (bf16[4,128,800]{1,2,0:T(8,128)(2,1)}, bf16[4,128,800]{1,2,0:T(8,128)(2,1)}, u32[]{:S(2)}, u32[]{:S(2)}) collective-permute-start(bf16[4,128,800]{1,2,0:T(8,128)(2,1)} %collective-permute-done.2), channel_id=1, source_target_pairs={{0,1},{1,2},{2,3},{3,4},{4,5},{5,6},{6,7},{7,8},{8,9},{9,10},{10,1... | collective-permute-start | bytes 2457608 | tf_op jit(solution)/shard_map/ppermute | solution.py:74
  72.2 3.9 copy-start.22
  72.2 15.1 %copy-start.21 = (s32[4]{0:T(128)S(1)}, s32[4]{0:T(128)}, u32[]{:S(2)}) copy-start(s32[4]{0:T(128)} %param.25) | copy-start | bytes 52
  72.2 25.0 %copy-start.17 = (s32[4,256]{1,0:T(4,128)S(1)}, s32[4,256]{1,0:T(4,128)}, u32[]{:S(2)}) copy-start(s32[4,256]{1,0:T(4,128)} %param.23) | copy-start | bytes 12292
  72.2 25.1 %copy-start.16 = (s32[4,256]{1,0:T(4,128)S(1)}, s32[4,256]{1,0:T(4,128)}, u32[]{:S(2)}) copy-start(s32[4,256]{1,0:T(4,128)} %param.22) | copy-start | bytes 12292
  72.2 35.4 %copy-start.15 = (bf16[512,800]{0,1:T(8,128)(2,1)S(1)}, bf16[512,800]{0,1:T(8,128)(2,1)}, u32[]{:S(2)}) copy-start(bf16[512,800]{0,1:T(8,128)(2,1)} %param.16) | copy-start | bytes 2457604
  76.3 21.1 %collective-permute-start.10 = (bf16[4,128,800]{1,2,0:T(8,128)(2,1)}, bf16[4,128,800]{1,2,0:T(8,128)(2,1)}, u32[]{:S(2)}, u32[]{:S(2)}) collective-permute-start(bf16[4,128,800]{1,2,0:T(8,128)(2,1)} %collective-permute-done.9), channel_id=1, source_target_pairs={{0,15},{1,0},{2,1},{3,2},{4,3},{5,4},{6,5},{7,6},{8,7},{9,8},{10,9... | collective-permute-start | bytes 2457608 | tf_op jit(solution)/shard_map/ppermute | solution.py:77
  87.3 20.2 %collective-permute-start.4 = (bf16[4,128,800]{1,2,0:T(8,128)(2,1)}, bf16[4,128,800]{1,2,0:T(8,128)(2,1)}, u32[]{:S(2)}, u32[]{:S(2)}) collective-permute-start(bf16[4,128,800]{1,2,0:T(8,128)(2,1)} %collective-permute-done.3), channel_id=1, source_target_pairs={{0,1},{1,2},{2,3},{3,4},{4,5},{5,6},{6,7},{7,8},{8,9},{9,10},{10,1... | collective-permute-start | bytes 2457608 | tf_op jit(solution)/shard_map/ppermute | solution.py:74
  88.6 211.3 %all-to-all-start = ((s32[16,1,2]{2,1,0:T(1,128)}), s32[16,1,2]{2,1,0:T(1,128)S(1)}, u32[]{:S(2)}, u32[]{:S(2)}) async-start(s32[16,1,2]{2,1,0:T(1,128)} %bitcast.13), calls=%async_computation | async-start | bytes 16384 | tf_op jit(solution)/shard_map/all_to_all | solution.py:165
  97.4 26.8 %collective-permute-start.11 = (bf16[4,128,800]{1,2,0:T(8,128)(2,1)}, bf16[4,128,800]{1,2,0:T(8,128)(2,1)}, u32[]{:S(2)}, u32[]{:S(2)}) collective-permute-start(bf16[4,128,800]{1,2,0:T(8,128)(2,1)} %collective-permute-done.10), channel_id=1, source_target_pairs={{0,15},{1,0},{2,1},{3,2},{4,3},{5,4},{6,5},{7,6},{8,7},{9,8},{10,9... | collective-permute-start | bytes 2457608 | tf_op jit(solution)/shard_map/ppermute | solution.py:77
  107.5 21.5 %collective-permute-start.5 = (bf16[4,128,800]{1,2,0:T(8,128)(2,1)}, bf16[4,128,800]{1,2,0:T(8,128)(2,1)}, u32[]{:S(2)}, u32[]{:S(2)}) collective-permute-start(bf16[4,128,800]{1,2,0:T(8,128)(2,1)} %collective-permute-done.4), channel_id=1, source_target_pairs={{0,1},{1,2},{2,3},{3,4},{4,5},{5,6},{6,7},{7,8},{8,9},{9,10},{10,1... | collective-permute-start | bytes 2457608 | tf_op jit(solution)/shard_map/ppermute | solution.py:74
  121.8 2.1 copy-start.5
  124.2 6.5 copy-start.1
  124.2 14.4 %collective-permute-start.12 = (bf16[4,128,800]{1,2,0:T(8,128)(2,1)}, bf16[4,128,800]{1,2,0:T(8,128)(2,1)}, u32[]{:S(2)}, u32[]{:S(2)}) collective-permute-start(bf16[4,128,800]{1,2,0:T(8,128)(2,1)} %collective-permute-done.11), channel_id=1, source_target_pairs={{0,15},{1,0},{2,1},{3,2},{4,3},{5,4},{6,5},{7,6},{8,7},{9,8},{10,9... | collective-permute-start | bytes 2457608 | tf_op jit(solution)/shard_map/ppermute | solution.py:77
  129.0 17.7 %collective-permute-start.6 = (bf16[4,128,800]{1,2,0:T(8,128)(2,1)}, bf16[4,128,800]{1,2,0:T(8,128)(2,1)}, u32[]{:S(2)}, u32[]{:S(2)}) collective-permute-start(bf16[4,128,800]{1,2,0:T(8,128)(2,1)} %collective-permute-done.5), channel_id=1, source_target_pairs={{0,1},{1,2},{2,3},{3,4},{4,5},{5,6},{6,7},{7,8},{8,9},{9,10},{10,1... | collective-permute-start | bytes 2457608 | tf_op jit(solution)/shard_map/ppermute | solution.py:74
  138.6 23.9 %collective-permute-start.13 = (bf16[4,128,800]{1,2,0:T(8,128)(2,1)}, bf16[4,128,800]{1,2,0:T(8,128)(2,1)S(1)}, u32[]{:S(2)}, u32[]{:S(2)}) collective-permute-start(bf16[4,128,800]{1,2,0:T(8,128)(2,1)} %collective-permute-done.12), channel_id=1, source_target_pairs={{0,15},{1,0},{2,1},{3,2},{4,3},{5,4},{6,5},{7,6},{8,7},{9,8},{10,9... | collective-permute-start | bytes 2457608 | tf_op jit(solution)/shard_map/ppermute | solution.py:77
  146.7 22.6 %collective-permute-start.7 = (bf16[4,128,800]{1,2,0:T(8,128)(2,1)}, bf16[4,128,800]{1,2,0:T(8,128)(2,1)S(1)}, u32[]{:S(2)}, u32[]{:S(2)}) collective-permute-start(bf16[4,128,800]{1,2,0:T(8,128)(2,1)} %collective-permute-done.6), channel_id=1, source_target_pairs={{0,1},{1,2},{2,3},{3,4},{4,5},{5,6},{6,7},{7,8},{8,9},{9,10},{10,1... | collective-permute-start | bytes 2457608 | tf_op jit(solution)/shard_map/ppermute | solution.py:74
  162.5 21.6 %collective-permute-start.14 = (bf16[4,128,800]{1,2,0:T(8,128)(2,1)S(1)}, bf16[4,128,800]{1,2,0:T(8,128)(2,1)S(1)}, u32[]{:S(2)}, u32[]{:S(2)}) collective-permute-start(bf16[4,128,800]{1,2,0:T(8,128)(2,1)S(1)} %collective-permute-done.13), channel_id=1, source_target_pairs={{0,15},{1,0},{2,1},{3,2},{4,3},{5,4},{6,5},{7,6},{8,7},{9,8},{10,9... | collective-permute-start | bytes 2457608 | tf_op jit(solution)/shard_map/ppermute | solution.py:77
  170.6 5.4 copy-start.12
  172.0 4.1 copy-start.8
  173.3 2.9 copy-start.2
  174.7 1.7 copy-start.10
  245.3 3.1 copy-start.4
  245.3 3.9 copy-start.23
  248.3 4.1 copy-start
  248.3 2.7 copy-start.13
  252.4 1.8 copy-start.14
  260.1 3.1 copy-start.4
  260.1 3.9 copy-start.23
  263.1 4.1 copy-start
  263.1 2.7 copy-start.13
  267.3 1.8 copy-start.14
  299.9 99.2 %all-to-all-start.1 = ((bf16[16,2,128,800]{2,3,1,0:T(8,128)(2,1)}), bf16[16,2,128,800]{2,3,1,0:T(8,128)(2,1)}, u32[]{:S(2)}, u32[]{:S(2)}) async-start(bf16[16,2,128,800]{2,3,1,0:T(8,128)(2,1)} %bitcast.86), calls=%async_computation.1 | async-start | bytes 13107200 | tf_op jit(solution)/shard_map/all_to_all | solution.py:164
  304.5 319.3 %all-reduce.8.cloned.1.call-start = ((), (), s32[]{:S(2)}) async-start(), calls=%async_computation.4 | async-start | bytes 6553600 | tf_op jit(solution)/shard_map/psum | solution.py:179
  315.9 1.1 copy-start.3
  315.9 2.4 copy-start.18
  315.9 424.6 %all-reduce.6.cloned.1.call-start = ((), (), s32[]{:S(2)}) async-start(), calls=%async_computation.3 | async-start | bytes 3276800 | tf_op jit(solution)/shard_map/psum | solution.py:37
  435.5 11.2 %copy-start.19 = (f32[512]{0:T(512)S(1)}, f32[512]{0:T(512)}, u32[]{:S(2)}) copy-start(f32[512]{0:T(512)} %param.17) | copy-start | bytes 6148
  748.7 3.3 copy-start.20
  748.7 3.9 copy-start.6
Sparse Core Ops, SparseCore 0:
  76.2 169.0 all-reduce.3
  316.0 307.7 all-reduce.7
  626.2 114.2 all-reduce.5
